TPU v7x, 32 devices: a whole 2x2x4 slice. The times are simulated.
32 devices in a mesh: groups: 2 (over x), span: 8 (over z, y), head: 2 (over core).
Axes of the slice: x: 2, y: 2, z: 4, core: 2. Of those that a mesh axis runs over, the one named last changes fastest.
Arguments:
- span_states: bfloat16 [2048, 4096], P(('groups', 'span'), 'head'), parts along dimension 0, may hold values from -1.5 to 1.5
- span_queries: bfloat16 [2048, 2048], P(('groups', 'span'), 'head'), parts along dimension 0, may hold values from -1000 to 1000
- span_memory: bfloat16 [2048, 2, 896], P(('groups', 'span'), None, 'head'), parts along dimension 0, may hold values from -1000 to 1000
- passages: bfloat16 [16384, 896], P(('groups', 'span')), parts along dimension 0, may hold values from -1.5 to 1.5
- neighbours: int32 [32, 2], P(('groups', 'span')), parts along dimension 0, may hold values from 0 to 63, as said below
- enc_query_w: bfloat16 [896, 896], P(None, 'head'), may hold values from -0.1875 to 0.1875
- enc_out_w: bfloat16 [896, 896], P(None, 'head'), may hold values from -0.1875 to 0.1875
- kv_weight: bfloat16 [896, 2, 2048], P(None, None, ('head', 'span')), may hold values from -0.1875 to 0.1875
- out_weight: bfloat16 [2048, 4096], P('head', 'span'), may hold values from -0.125 to 0.125
Outputs:
- mixed_states: bfloat16 [2048, 4096], P(('groups', 'span'), 'head'), parts along dimension 0
There are 2 independent parts, one for each index of `groups`. A program takes and returns all parts, laid end to end along the dimension named above; an argument that names none is the same for every part. Nothing has to cross between parts.
Inputs may be any that keep to these rules, and one draw needn't show every extreme that they name: `neighbours`: passage p belongs to index p // 8 of the span axis. Among the spans of one index of the span axis, all 4 passages listed belong to distinct indices.
All inputs are finite; a program needn't handle non-finite values.
Results may differ from a plain program's by a relative error of at most 0.025.
Values may be sent and summed in bfloat16 or wider, within the bound.
A program may use at most 64 MiB of HBM per device.

v0:
```python
import math

import jax
import jax.numpy as jnp
from jax import lax
from jax.sharding import PartitionSpec as P

HD = 128
E = 896
EHD = 64
CT = 64
PT = 128
NB = 2
PS_DEV = 8


epsilon = 1e-06


def rms_rows(values):
    return values * lax.rsqrt(jnp.mean(values * values, axis=-1, keepdims=True) + epsilon)


def softmax_rows(scores):
    top_score = jnp.max(scores, axis=-1, keepdims=True)
    raised = jnp.exp(scores - top_score)
    return raised / jnp.sum(raised, axis=-1, keepdims=True)


def wanted_slots(owner_flat, local_flat, device_count):
    matched = owner_flat[:, None] == jnp.arange(device_count, dtype=jnp.int32)[None, :]
    return jnp.sum(jnp.where(matched, local_flat[:, None], 0), axis=0)


def fetch_passages(wanted, passages):
    blocks = passages.reshape(-1, PT, E)
    picked = blocks[lax.all_to_all(wanted, "span", split_axis=0, concat_axis=0, tiled=True)]
    return lax.all_to_all(picked, "span", split_axis=0, concat_axis=0, tiled=True)


def encode_branch(copies, memory, query_w, out_w):
    groups = copies.shape[0]
    span_count = copies.shape[1]
    head_count = memory.shape[3]
    flat_rows = copies.reshape(-1, E).astype(jnp.float32)
    normed = rms_rows(flat_rows).astype(jnp.bfloat16)
    enc_query = jnp.dot(normed, query_w, preferred_element_type=jnp.float32).astype(jnp.bfloat16)
    enc_query = enc_query.reshape(groups, span_count, PT, head_count, EHD)
    scores = jnp.einsum(
        "gcqhd,ckhd->gchqk", enc_query, memory[:, :, 0], preferred_element_type=jnp.float32
    ) / math.sqrt(EHD)
    weights = softmax_rows(scores).astype(jnp.bfloat16)
    mixed_heads = jnp.einsum(
        "gchqk,ckhd->gcqhd", weights, memory[:, :, 1], preferred_element_type=jnp.float32
    )
    mixed_heads = mixed_heads.astype(jnp.bfloat16).reshape(-1, head_count * EHD)
    branch = lax.dot_general(
        mixed_heads, out_w, (((1,), (1,)), ((), ())), preferred_element_type=jnp.float32
    )
    return (flat_rows, branch)


def body(
    span_states,
    span_queries,
    span_memory,
    passages,
    neighbours,
    enc_query_w,
    enc_out_w,
    kv_weight,
    out_weight,
):
    device_count = lax.axis_size("span")
    head_index = lax.axis_index("head")
    span_count = neighbours.shape[0]
    owners = neighbours // PS_DEV
    local_ids = neighbours % PS_DEV
    wanted = wanted_slots(owners.reshape(-1), local_ids.reshape(-1), device_count)[:, None]
    fetched = fetch_passages(wanted, passages)
    own_owner = lax.dynamic_index_in_dim(owners, head_index, 1, keepdims=False)
    copies = fetched[own_owner, 0][None]
    query_full, out_full = (
        lax.all_gather(enc_query_w, "head", axis=1, tiled=True),
        lax.all_gather(enc_out_w, "head", axis=1, tiled=True),
    )
    memory_full = lax.all_gather(span_memory, "head", axis=2, tiled=True)
    memory = memory_full.reshape(span_count, CT, 2, -1, EHD)
    own_rows, own_branch = encode_branch(copies, memory, query_full, out_full)
    encoded = rms_rows(own_rows + own_branch).astype(jnp.bfloat16)
    all_encoded = lax.all_gather(encoded[None], "head", axis=0, tiled=True)
    flat_encoded = all_encoded.reshape(-1, E)
    dec_kv = jnp.einsum(
        "re,esc->rsc",
        flat_encoded,
        lax.all_gather(kv_weight, "span", axis=2, tiled=True),
        preferred_element_type=jnp.float32,
    ).astype(jnp.bfloat16)
    head_count = span_queries.shape[1] // HD
    dec_kv = dec_kv.reshape(NB, span_count, PT, 2, head_count, HD)
    dec_query = span_queries.reshape(span_count, CT, head_count, HD)
    scores = jnp.einsum(
        "cqhd,ncphd->chqnp", dec_query, dec_kv[:, :, :, 0], preferred_element_type=jnp.float32
    ) / math.sqrt(HD)
    scores = scores.reshape(span_count, head_count, CT, NB * PT)
    weights = softmax_rows(scores).astype(jnp.bfloat16).reshape(span_count, head_count, CT, NB, PT)
    attended = jnp.einsum(
        "chqnp,ncphd->cqhd", weights, dec_kv[:, :, :, 1], preferred_element_type=jnp.float32
    )
    attended = attended.astype(jnp.bfloat16).reshape(span_count * CT, head_count * HD)
    partial_value = jnp.dot(
        attended,
        lax.all_gather(out_weight, "span", axis=1, tiled=True),
        preferred_element_type=jnp.float32,
    )
    summed = lax.psum_scatter(
        partial_value.astype(jnp.bfloat16), "head", scatter_dimension=1, tiled=True
    ).astype(jnp.float32)
    return (span_states.astype(jnp.float32) + summed).astype(jnp.bfloat16)


def solution(mesh):
    placed = (
        P(("groups", "span"), "head"),
        P(("groups", "span"), "head"),
        P(("groups", "span"), None, "head"),
        P(("groups", "span"), None),
        P(("groups", "span"), None),
        P(None, "head"),
        P(None, "head"),
        P(None, None, ("head", "span")),
        P("head", "span"),
    )
    return jax.shard_map(
        body, mesh=mesh, in_specs=placed, out_specs=P(("groups", "span"), "head"), check_vma=False
    )
```

profile of v0, /device:TPU:1, one launch (start us, length us, event | category | flops | bytes accessed | tf_op | source)
XLA Modules:
  0.0 270.5 jit_solution(14112811568693671814)
XLA Ops:
  6.5 0.7 all-gather.6.cloned.1.call-update
  7.3 0.7 all-gather.8.cloned.1.call-update
  8.1 0.8 copy.54
  9.9 11.5 %all_to_all.14 = s32[8,1,1]{2,1,0:T(1,128)S(1)} all-to-all(s32[8,1,1]{2,1,0:T(1,128)S(1)} %copy.48), channel_id=1, replica_groups=mesh['groups'=2,'span'=8,'head'=2] {'span'}, dimensions={0} | all-to-all | bytes 64 | tf_op jit(solution)/shard_map/all_to_all | solution.py:37
  21.6 2.0 gather_fusion
  23.6 4.4 %all-to-all-start.1 = ((bf16[8,1,128,896]{3,2,1,0:T(8,128)(2,1)}), bf16[8,1,128,896]{3,2,1,0:T(8,128)(2,1)}, u32[]{:S(2)}, u32[]{:S(2)}) async-start(bf16[8,1,128,896]{3,2,1,0:T(8,128)(2,1)} %bitcast.92), calls=%async_computation.1 | async-start | bytes 3670016 | tf_op jit(solution)/shard_map/all_to_all | solution.py:38
  28.1 3.9 %all_gather.19 = bf16[128,2,896]{0,2,1:T(8,128)(2,1)S(1)} all-gather(bf16[128,2,448]{0,2,1:T(8,128)(2,1)S(1)} %copy-done.6), channel_id=1, replica_groups=mesh['groups'=2,'span'=8,'head'=2] {'head'}, dimensions={2}, use_global_device_ids=true | all-gather | bytes 688128 | tf_op jit(solution)/shard_map/all_gather | solution.py:87
  32.4 1.7 fusion.25
  34.1 1.1 copy.66
  35.4 0.7 bitcast_bitcast_fusion
  36.2 46.8 %all-to-all-done.1 = bf16[8,1,128,896]{3,2,1,0:T(8,128)(2,1)} async-done(((bf16[8,1,128,896]{3,2,1,0:T(8,128)(2,1)}), bf16[8,1,128,896]{3,2,1,0:T(8,128)(2,1)}, u32[]{:S(2)}, u32[]{:S(2)}) %all-to-all-start.1) | async-done | bytes 1835040 | tf_op jit(solution)/shard_map/all_to_all | solution.py:38
  83.0 2.1 gather_fusion.1
  85.5 2.9 %convolution_convert_fusion.3 = bf16[256,896]{1,0:T(8,128)(2,1)} fusion(bf16[256,896]{1,0:T(8,128)(2,1)S(1)} %fusion.8, bf16[896,896]{0,1:T(8,128)(2,1)} %all-gather.6.cloned.1.call-done), kind=kOutput, calls=%fused_computation.10 | convolution fusion | flops 411271168 | bytes 2523136 | tf_op jit(solution)/shard_map/dot_general | solution.py:47
  88.4 1.8 reshape.118
  90.2 1.8 fusion.26
  93.1 2.3 multiply_reduce_fusion
  95.5 5.5 %all-gather = bf16[512,896]{1,0:T(8,128)(2,1)S(1)} all-gather(bf16[256,896]{1,0:T(8,128)(2,1)S(1)} %multiply_convert_fusion), channel_id=2, replica_groups=mesh['groups'=2,'span'=8,'head'=2] {'head'}, dimensions={0}, use_global_device_ids=true | all-gather | bytes 1376256 | tf_op jit(solution)/shard_map/all_gather | solution.py:91
  101.0 22.2 %all-gather.10.cloned.1.call-done = bf16[896,2,1024]{2,0,1:T(8,128)(2,1)} async-done(((bf16[896,2,128]{2,0,1:T(8,128)(2,1)}), bf16[896,2,1024]{2,0,1:T(8,128)(2,1)}) %all-gather.10.cloned.1.call-update) | async-done | bytes 3670032 | tf_op jit(solution)/shard_map/all_gather | solution.py:96
  123.1 4.4 %convolution_convert_fusion.1 = bf16[512,2,1024]{2,0,1:T(8,128)(2,1)S(1)} fusion(bf16[896,2,1024]{2,0,1:T(8,128)(2,1)} %all-gather.10.cloned.1.call-done, bf16[512,896]{1,0:T(8,128)(2,1)S(1)} %all-gather), kind=kOutput, calls=%fused_computation.3 | convolution fusion | flops 1880096768 | bytes 6684672 | tf_op jit(solution)/shard_map/re,esc->rsc/dot_general | solution.py:93
  128.3 0.8 copy-done.1
  130.8 117.5 %all-gather.12.cloned.1.call-done = bf16[1024,4096]{1,0:T(8,128)(2,1)} async-done(((bf16[1024,512]{1,0:T(8,128)(2,1)}), bf16[1024,4096]{1,0:T(8,128)(2,1)}) %all-gather.12.cloned.1.call-update) | async-done | bytes 8388624 | tf_op jit(solution)/shard_map/all_gather | solution.py:113
  248.3 5.8 %convolution_convert_fusion = bf16[128,4096]{1,0:T(8,128)(2,1)} fusion(bf16[1024,4096]{1,0:T(8,128)(2,1)} %all-gather.12.cloned.1.call-done, bf16[16,8,8,128]{3,2,1,0:T(8,128)(2,1)S(1)} %bitcast.95), kind=kOutput, calls=%fused_computation.2 | convolution fusion | flops 1074266112 | bytes 9699328 | tf_op jit(solution)/shard_map/dot_general | solution.py:111
  254.1 7.9 %reduce-scatter.2.cloned.1.call-done = bf16[128,2048]{1,0:T(8,128)(2,1)} async-done(((bf16[128,4096]{1,0:T(8,128)(2,1)}), bf16[128,2048]{1,0:T(8,128)(2,1)}) %reduce-scatter.2.cloned.1.call-update) | async-done | bytes 524304 | tf_op jit(solution)/shard_map/reduce_scatter | solution.py:116
  262.0 2.0 add_convert_fusion
  (49 shorter events, 5.8 us)
Async XLA Ops:
  6.5 15.1 %copy-start = (bf16[1024,896]{1,0:T(8,128)(2,1)S(1)}, bf16[1024,896]{1,0:T(8,128)(2,1)}, u32[]{:S(2)}) copy-start(bf16[1024,896]{1,0:T(8,128)(2,1)} %param.12) | copy-start | bytes 5505028
  6.5 1.5 copy-start.4
  6.5 3.0 %copy-start.7 = (s32[2,2]{1,0:T(2,128)S(1)}, s32[2,2]{1,0:T(2,128)}, u32[]{:S(2)}) copy-start(s32[2,2]{1,0:T(2,128)} %param.13) | copy-start | bytes 52
  6.5 78.9 %all-gather.6.cloned.1.call-start = ((), (), s32[]{:S(2)}) async-start(), calls=%async_computation.3 | async-start | bytes 2408448 | tf_op jit(solution)/shard_map/all_gather | solution.py:84
  7.3 85.8 %all-gather.8.cloned.1.call-start = ((), (), s32[]{:S(2)}) async-start(), calls=%async_computation.4 | async-start | bytes 2408448 | tf_op jit(solution)/shard_map/all_gather | solution.py:85
  8.0 115.1 %all-gather.10.cloned.1.call-start = ((), (), s32[]{:S(2)}) async-start(), calls=%async_computation.5 | async-start | bytes 4128768 | tf_op jit(solution)/shard_map/all_gather | solution.py:96
  8.9 239.4 %all-gather.12.cloned.1.call-start = ((), (), s32[]{:S(2)}) async-start(), calls=%async_computation.6 | async-start | bytes 9437184 | tf_op jit(solution)/shard_map/all_gather | solution.py:113
  23.6 4.5 %copy-start.6 = (bf16[128,2,448]{0,2,1:T(8,128)(2,1)S(1)}, bf16[128,2,448]{0,2,1:T(8,128)(2,1)}, u32[]{:S(2)}) copy-start(bf16[128,2,448]{0,2,1:T(8,128)(2,1)} %param.11) | copy-start | bytes 688132
  23.6 59.4 %all-to-all-start.1 = ((bf16[8,1,128,896]{3,2,1,0:T(8,128)(2,1)}), bf16[8,1,128,896]{3,2,1,0:T(8,128)(2,1)}, u32[]{:S(2)}, u32[]{:S(2)}) async-start(bf16[8,1,128,896]{3,2,1,0:T(8,128)(2,1)} %bitcast.92), calls=%async_computation.1 | async-start | bytes 3670016 | tf_op jit(solution)/shard_map/all_to_all | solution.py:38
  28.1 233.9 %reduce-scatter.2.cloned.1.call-start = ((), (), s32[]{:S(2)}) async-start(), calls=%async_computation.7 | async-start | bytes 1572864 | tf_op jit(solution)/shard_map/reduce_scatter | solution.py:116
  32.0 3.2 %copy-start.5 = (bf16[128,1024]{1,0:T(8,128)(2,1)S(1)}, bf16[128,1024]{1,0:T(8,128)(2,1)}, u32[]{:S(2)}) copy-start(bf16[128,1024]{1,0:T(8,128)(2,1)} %param.10) | copy-start | bytes 786436
  90.2 2.0 copy-start.3
  128.2 1.0 copy-start.1
  248.3 13.7 %copy-start.2 = (bf16[128,2048]{1,0:T(8,128)(2,1)S(1)}, bf16[128,2048]{1,0:T(8,128)(2,1)}, u32[]{:S(2)}) copy-start(bf16[128,2048]{1,0:T(8,128)(2,1)} %param.9) | copy-start | bytes 1572868
Sparse Core Ops, SparseCore 0:
  8.9 12.2 all-gather.5
  22.8 11.0 all-gather.7
  35.9 87.2 all-gather.9
  125.0 123.2 all-gather.11
  254.2 7.7 reduce-scatter.1
where the time goes:
time: 271 us; the launch traced here: 270 us
  waiting for transfers between devices  196 us (72%)
  blocking collectives  20.9 us (8%)
  matrix products  18.5 us (7%)
  between operations  13.4 us (5%)
  local copies, waits for them, and re-layouts  13.1 us (5%)
  starting transfers between devices  4.61 us (2%)
  other arithmetic  3.53 us (1%)
    all_gather x1, waiting for transfers between devices, body(): lax.all_gather(out_weight, 'span', axis=1, tiled=True)  118 us
    all_to_all x1, waiting for transfers between devices, fetch_passages(): lax.all_to_all(picked, 'span', split_axis=0, concat_axis=0, tiled=True)  46.8 us
    all_gather x1, waiting for transfers between devices, body(): lax.all_gather(kv_weight, 'span', axis=2, tiled=True)  22.2 us
    all_to_all x1, blocking collectives, fetch_passages(): lax.all_to_all(wanted, 'span', split_axis=0, concat_axis=0, tiled=True)  11.5 us
    reduce_scatter x1, waiting for transfers between devices, body(): lax.psum_scatter(partial_value.astype(jnp.bfloat16), 'head', scatter_dime...  7.88 us
    dot_general x1, matrix products, body(): jnp.dot(attended, lax.all_gather(out_weight, 'span', axis=1, tiled=True),...  5.75 us
    all_gather x1, blocking collectives, body(): all_encoded = lax.all_gather(encoded[None], 'head', axis=0, tiled=True)  5.52 us
  transfers between devices with their start and end apart: 6, of which 4 were waited for; matrix products, arithmetic and copies ran while one was open for 10% of the time, Pallas kernels for 0%

commit v1 on v0

v1 whole, which is shorter than its diff:
```python
import functools
import math

import jax
import jax.numpy as jnp
from jax import lax
from jax.experimental import pallas as pl
from jax.experimental.pallas import tpu as pltpu
from jax.sharding import PartitionSpec as P

HD = 128
E = 896
EHD = 64
CT = 64
PT = 128
NB = 2
PS_DEV = 8
MESH = pl.DeviceIdType.MESH


epsilon = 1e-06


def rms_rows(values):
    return values * lax.rsqrt(jnp.mean(values * values, axis=-1, keepdims=True) + epsilon)


def softmax_rows(scores):
    top_score = jnp.max(scores, axis=-1, keepdims=True)
    raised = jnp.exp(scores - top_score)
    return raised / jnp.sum(raised, axis=-1, keepdims=True)


def ring_place(span, n):
    odd = span % 2
    return (1 - odd) * (span // 2) + odd * (n - 1 - span // 2)


def ring_span(place, n):
    back = place // (n // 2)
    return (1 - back) * (2 * place) + back * (2 * (n - 1 - place) + 1)


def remote(src, dst, send_sem, recv_sem, **where):
    return pltpu.make_async_remote_copy(
        src_ref=src, dst_ref=dst, send_sem=send_sem, recv_sem=recv_sem,
        device_id=where, device_id_type=MESH,
    )


class Ring:
    def __init__(self, n, own, out, halves, sems):
        me = lax.axis_index("span")
        self.n, self.own, self.out, self.halves, self.sems = n, own, out, halves, sems
        self.place = ring_place(me, n)
        self.right = ring_span((self.place + 1) % n, n)
        self.left = ring_span((self.place + n - 1) % n, n)
        self.steps = n // 2
        self.copies = []

    def start(self, t):
        n = self.n
        pair = []
        for side, target in ((0, self.right), (1, self.left)):
            place = (self.place + (n - t if side == 0 else t)) % n
            block = ring_span(place, n)
            src = self.own if t == 0 else self.out.at[block]
            dst = self.out.at[block]
            if t == self.steps - 1:
                src, dst = self.halves(src, side), self.halves(dst, side)
            copy = remote(src, dst, self.sems.at[0, side, t], self.sems.at[1, side, t], span=target)
            copy.start()
            pair.append(copy)
        self.copies.append(pair)

    def arrived(self, t):
        for copy in self.copies[t]:
            copy.wait_recv()
        n = self.n
        blocks = [ring_span((self.place + n - t - 1) % n, n), ring_span((self.place + t + 1) % n, n)]
        return blocks[:1] if t == self.steps - 1 else blocks

    def finish(self):
        for pair in self.copies:
            for copy in pair:
                copy.wait_send()


def fetch_kernel(
    n, spans, nb_ref, pas_ref, mem_ref, wq_ref, wo_ref, kv_ref,
    cop_ref, memo_ref, wqo_ref, woo_ref, kvg_ref,
    nbg, nbs, picks, got, swap, local_sem, nb_sem, pas_sem, swap_sem, w_sem, ring_sem,
):
    me = lax.axis_index("span")
    head = lax.axis_index("head")
    other = 1 - head
    barrier = pltpu.get_barrier_semaphore()
    for d in range(1, n):
        pl.semaphore_signal(barrier, inc=1, device_id={"span": (me + d) % n}, device_id_type=MESH)
    pl.semaphore_signal(barrier, inc=1, device_id={"head": other}, device_id_type=MESH)
    pl.semaphore_wait(barrier, n)

    nb_copies = []
    for d in range(1, n):
        copy = remote(nb_ref, nbg.at[me], nb_sem.at[0, d], nb_sem.at[1, d], span=(me + d) % n)
        copy.start()
        nb_copies.append(copy)
    own_nb = pltpu.make_async_copy(nb_ref, nbg.at[me], local_sem.at[0])
    own_nb.start()
    w_copies = [
        remote(src, dst, w_sem.at[0, i], w_sem.at[1, i], head=other)
        for i, (src, dst) in enumerate(((mem_ref, memo_ref), (wq_ref, wqo_ref), (wo_ref, woo_ref)))
    ]
    for copy in w_copies:
        copy.start()
    own_kv = pltpu.make_async_copy(kv_ref, kvg_ref.at[me], local_sem.at[1])
    own_kv.start()
    own_nb.wait()
    for copy in nb_copies:
        copy.wait()
    to_scalar = pltpu.make_async_copy(nbg, nbs, local_sem.at[2])
    to_scalar.start()
    to_scalar.wait()

    def pick(requester):
        index = jnp.int32(0)
        for e in range(spans * NB):
            wanted = nbs[requester, 0, e]
            index = index + jnp.where(wanted // PS_DEV == me, wanted % PS_DEV, 0)
        return pas_ref[index, head]

    pas_copies = []
    picks[1] = pick((me + 1) % n)
    for d in range(1, n):
        if d + 1 < n:
            picks[d + 1] = pick((me + d + 1) % n)
        else:
            got[me] = pick(me)
        copy = remote(picks.at[d], got.at[me], pas_sem.at[0, d], pas_sem.at[1, d], span=(me + d) % n)
        copy.start()
        pas_copies.append(copy)

    ring = Ring(n, kv_ref, kvg_ref, lambda ref, side: ref.at[side], ring_sem)
    ring.start(0)
    for copy in pas_copies:
        copy.wait_recv()
    swaps = []
    for c in range(spans):
        swap[c] = got[nbs[me, 0, c * NB + other] // PS_DEV]
    for c in range(spans):
        cop_ref[c, head] = got[nbs[me, 0, c * NB + head] // PS_DEV]
        copy = remote(swap.at[c], cop_ref.at[c, head], swap_sem.at[0, c], swap_sem.at[1, c], head=other)
        copy.start()
        swaps.append(copy)
    for t in range(ring.steps):
        ring.arrived(t)
        if t + 1 < ring.steps:
            ring.start(t + 1)
    own_kv.wait()
    for copy in swaps + w_copies:
        copy.wait()
    for copy in pas_copies:
        copy.wait_send()
    ring.finish()


def out_kernel(
    n, att_ref, w_ref, states_ref, out_ref,
    gathered, part, crossed, summed, back, ring_sem, cross_sem, send_sem, back_sem, local_sem,
):
    me = lax.axis_index("span")
    head = lax.axis_index("head")
    other = 1 - head
    half = n // 2
    owner_head = me // half
    column = me % half
    rows = att_ref.shape[0]
    half_rows = rows // 2
    width = w_ref.shape[1]
    barrier = pltpu.get_barrier_semaphore()
    for d in range(n):
        for hop in range(2):
            if d or hop:
                pl.semaphore_signal(
                    barrier, inc=1,
                    device_id={"span": (me + d) % n, "head": (head + hop) % 2}, device_id_type=MESH,
                )
    pl.semaphore_wait(barrier, 2 * n - 1)

    ring = Ring(n, att_ref, gathered, lambda ref, side: ref.at[pl.ds(side * half_rows, half_rows)], ring_sem)
    ring.start(0)
    crossings, returns = [], []

    def project(block, rows_ref):
        i = len(crossings)
        value = jnp.dot(rows_ref[...], w_ref[...], preferred_element_type=jnp.float32)
        value = value.astype(jnp.bfloat16)
        part[i, 0] = value[:half_rows]
        part[i, 1] = value[half_rows:]
        copy = remote(part.at[i, other], crossed.at[i], cross_sem.at[0, i], cross_sem.at[1, i], head=other)
        crossings.append((copy, block))

    def send_across():
        crossings[-1][0].start()

    def give_back():
        i = len(returns)
        copy, block = crossings[i]
        copy.wait_recv()
        total = part[i, head].astype(jnp.float32) + crossed[i].astype(jnp.float32)
        summed[i] = total.astype(jnp.bfloat16)
        copy = remote(
            summed.at[i], back.at[column, head], send_sem.at[i], back_sem.at[column, head],
            span=block, head=owner_head,
        )
        if i == 0:
            @pl.when(head != owner_head)
            def _():
                copy.start()

            @pl.when(head == owner_head)
            def _():
                back[column, head] = summed[i]
        else:
            copy.start()
        returns.append(copy)

    project(me, att_ref)
    send_across()
    for t in range(ring.steps):
        blocks = ring.arrived(t)
        if t + 1 < ring.steps:
            ring.start(t + 1)
        for block in blocks:
            project(block, gathered.at[block])
            send_across()
            give_back()
    give_back()

    for j in range(half):
        for source in range(2):
            mine = (head * half + j == me) & (head == source)

            @pl.when(jnp.logical_not(mine))
            def _():
                remote(
                    summed.at[0], back.at[j, source], send_sem.at[0], back_sem.at[j, source], head=other,
                ).wait_recv()

            lanes = pl.ds(j * width, width)
            lines = pl.ds(source * half_rows, half_rows)
            out_ref[lines, lanes] = (
                states_ref[lines, lanes].astype(jnp.float32) + back[j, source].astype(jnp.float32)
            ).astype(jnp.bfloat16)
    ring.finish()
    for copy, _ in crossings:
        copy.wait_send()
    for i, copy in enumerate(returns):
        if i == 0:
            @pl.when(head != owner_head)
            def _():
                copy.wait_send()
        else:
            copy.wait_send()


def vmem_call(kernel, collective_id, out_shape, scratch_shapes, *operands):
    outs = out_shape if isinstance(out_shape, (list, tuple)) else [out_shape]
    specs = [pl.BlockSpec(memory_space=pltpu.VMEM)] * len(outs)
    return pl.pallas_call(
        kernel,
        out_shape=out_shape,
        in_specs=[pl.BlockSpec(memory_space=pltpu.VMEM)] * len(operands),
        out_specs=specs if isinstance(out_shape, (list, tuple)) else specs[0],
        scratch_shapes=scratch_shapes,
        compiler_params=pltpu.CompilerParams(collective_id=collective_id, has_side_effects=True),
    )(*operands)


def encode_branch(copies, memory, query_w, out_w):
    span_count = copies.shape[0]
    head_count = memory.shape[3]
    flat_rows = copies.reshape(-1, E).astype(jnp.float32)
    normed = rms_rows(flat_rows).astype(jnp.bfloat16)
    enc_query = jnp.dot(normed, query_w, preferred_element_type=jnp.float32).astype(jnp.bfloat16)
    enc_query = enc_query.reshape(span_count, PT, head_count, EHD)
    scores = jnp.einsum(
        "cqhd,ckhd->chqk", enc_query, memory[:, :, 0], preferred_element_type=jnp.float32
    ) / math.sqrt(EHD)
    weights = softmax_rows(scores).astype(jnp.bfloat16)
    mixed_heads = jnp.einsum(
        "chqk,ckhd->cqhd", weights, memory[:, :, 1], preferred_element_type=jnp.float32
    )
    mixed_heads = mixed_heads.astype(jnp.bfloat16).reshape(-1, head_count * EHD)
    branch = lax.dot_general(
        mixed_heads, out_w, (((1,), (1,)), ((), ())), preferred_element_type=jnp.float32
    )
    return (flat_rows, branch)


def body(
    span_states,
    span_queries,
    span_memory,
    passages,
    neighbours,
    enc_query_w,
    enc_out_w,
    kv_weight,
    out_weight,
):
    n = lax.axis_size("span")
    span_count = neighbours.shape[0]
    bf16 = jnp.bfloat16
    dma = pltpu.SemaphoreType.DMA
    half_rows = PT // 2
    flat_nb = neighbours.reshape(1, -1)
    nb = jnp.pad(flat_nb, ((0, 7), (0, 128 - flat_nb.shape[1])))
    kv = kv_weight.transpose(1, 0, 2)
    memory_flat = span_memory.reshape(span_memory.shape[0], -1)
    sds = jax.ShapeDtypeStruct
    copies, memory_other, query_other, out_other, kv_all = vmem_call(
        functools.partial(fetch_kernel, n, span_count), 0,
        [
            sds((span_count, 2, half_rows, E), bf16),
            sds(memory_flat.shape, bf16),
            sds(enc_query_w.shape, bf16),
            sds(enc_out_w.shape, bf16),
            sds((n,) + kv.shape, bf16),
        ],
        [
            pltpu.VMEM((n, 8, 128), jnp.int32),
            pltpu.SMEM((n, 8, 128), jnp.int32),
            pltpu.VMEM((n, half_rows, E), bf16),
            pltpu.VMEM((n, half_rows, E), bf16),
            pltpu.VMEM((span_count, half_rows, E), bf16),
            dma((3,)),
            dma((2, n)),
            dma((2, n)),
            dma((2, span_count)),
            dma((2, 3)),
            dma((2, 2, n // 2)),
        ],
        nb, passages.reshape(-1, 2, half_rows, E), memory_flat, enc_query_w, enc_out_w, kv,
    )
    query_full = jnp.concatenate([enc_query_w, query_other], axis=1)
    out_full = jnp.concatenate([enc_out_w, out_other], axis=1)
    memory = jnp.concatenate([span_memory, memory_other.reshape(span_memory.shape)], axis=2)
    memory = memory.reshape(span_count, CT, 2, -1, EHD)
    own_rows, own_branch = encode_branch(copies, memory, query_full, out_full)
    encoded = rms_rows(own_rows + own_branch).astype(bf16)
    all_encoded = lax.all_gather(encoded[None], "head", axis=0, tiled=True)
    flat_encoded = all_encoded.reshape(-1, E)
    dec_kv = jnp.einsum(
        "re,nsec->rsnc", flat_encoded, kv_all, preferred_element_type=jnp.float32
    ).astype(bf16)
    head_count = span_queries.shape[1] // HD
    dec_kv = dec_kv.reshape(NB, span_count, PT, 2, head_count, HD)
    dec_query = span_queries.reshape(span_count, CT, head_count, HD)
    scores = jnp.einsum(
        "cqhd,ncphd->chqnp", dec_query, dec_kv[:, :, :, 0], preferred_element_type=jnp.float32
    ) / math.sqrt(HD)
    scores = scores.reshape(span_count, head_count, CT, NB * PT)
    weights = softmax_rows(scores).astype(bf16).reshape(span_count, head_count, CT, NB, PT)
    attended = jnp.einsum(
        "chqnp,ncphd->cqhd", weights, dec_kv[:, :, :, 1], preferred_element_type=jnp.float32
    )
    attended = attended.astype(bf16).reshape(span_count * CT, head_count * HD)
    rows, width = attended.shape[0], out_weight.shape[1]
    return vmem_call(
        functools.partial(out_kernel, n), 1,
        sds(span_states.shape, bf16),
        [
            pltpu.VMEM((n,) + attended.shape, bf16),
            pltpu.VMEM((n, 2, rows // 2, width), bf16),
            pltpu.VMEM((n, rows // 2, width), bf16),
            pltpu.VMEM((n, rows // 2, width), bf16),
            pltpu.VMEM((n // 2, 2, rows // 2, width), bf16),
            dma((2, 2, n // 2)),
            dma((2, n)),
            dma((n,)),
            dma((n // 2, 2)),
            dma((1,)),
        ],
        attended, out_weight, span_states,
    )


def solution(mesh):
    placed = (
        P(("groups", "span"), "head"),
        P(("groups", "span"), "head"),
        P(("groups", "span"), None, "head"),
        P(("groups", "span"), None),
        P(("groups", "span"), None),
        P(None, "head"),
        P(None, "head"),
        P(None, None, ("head", "span")),
        P("head", "span"),
    )
    return jax.shard_map(
        body, mesh=mesh, in_specs=placed, out_specs=P(("groups", "span"), "head"), check_vma=False
    )
```

time: 271 us -> 152 us (0.56)
  waiting for transfers between devices: 196 us -> 0 us
  Pallas kernels: 0 us -> 111 us
  blocking collectives: 20.9 us -> 6.02 us
  between operations: 13.4 us -> 0.24 us
  matrix products: 18.5 us -> 10.3 us
  local copies, waits for them, and re-layouts: 13.1 us -> 21.1 us
  starting transfers between devices: 4.61 us -> 0 us
    all_gather x4 -> x0, waiting for transfers between devices: 140 us -> none  [the longest x1 118 us: body(): lax.all_gather(out_weight, 'span', axis=1, tiled=True)]
    pallas_call x0 -> x2, Pallas kernels: none -> 111 us  [vmem_call(): pl.pallas_call(kernel, out_shape=out_shape, in_specs=[pl.BlockSpec(memory...]
    all_to_all x1 -> x0, waiting for transfers between devices: 46.8 us -> none  [fetch_passages(): lax.all_to_all(picked, 'span', split_axis=0, concat_axis=0, tiled=True)]
    all_to_all x1 -> x0, blocking collectives: 11.5 us -> none  [fetch_passages(): lax.all_to_all(wanted, 'span', split_axis=0, concat_axis=0, tiled=True)]
    unnamed x20 -> x29, local copies, waits for them, and re-layouts: 3.4 us -> 11.7 us
    reduce_scatter x1 -> x0, waiting for transfers between devices: 7.88 us -> none  [body(): lax.psum_scatter(partial_value.astype(jnp.bfloat16), 'head', scatter_dime...]
    dot_general x4 -> x3, matrix products: 12.3 us -> 4.87 us  [the longest x1 3.77 us: body(): jnp.einsum('re,nsec->rsnc', flat_encoded, kv_all, preferred_element_type=...]
    all_to_all x1 -> x0, starting transfers between devices: 4.45 us -> none  [fetch_passages(): lax.all_to_all(picked, 'span', split_axis=0, concat_axis=0, tiled=True)]
  transfers between devices with their start and end apart: 6 -> 0, of which waited for: 4 -> 0; matrix products, arithmetic and copies ran while one was open for 10% -> 0% of each run, Pallas kernels for 0% -> 0%
where the time goes in v1:
time: 152 us
  Pallas kernels  111 us (73%)
  local copies, waits for them, and re-layouts  21.1 us (14%)
  matrix products  10.3 us (7%)
  blocking collectives  6.02 us (4%)
  other arithmetic  3.14 us (2%)
    pallas_call x2, Pallas kernels, vmem_call(): pl.pallas_call(kernel, out_shape=out_shape, in_specs=[pl.BlockSpec(memory...  111 us
    unnamed x29, local copies, waits for them, and re-layouts  11.7 us
    all_gather x1, blocking collectives, body(): all_encoded = lax.all_gather(encoded[None], 'head', axis=0, tiled=True)  6.02 us
    dot_general x1, matrix products, body(): jnp.einsum('re,nsec->rsnc', flat_encoded, kv_all, preferred_element_type=...  3.77 us

profile of v1, /device:TPU:1, one launch (start us, length us, event | category | flops | bytes accessed | tf_op | source)
XLA Modules:
  0.0 151.5 jit_solution(11932371949144494882)
XLA Ops:
  0.0 2.4 %copy.26.wq_ref = bf16[896,448]{1,0:T(8,128)(2,1)} copy(bf16[896,448]{0,1:T(8,128)(2,1)} %param.14) | data formatting | bytes 1605632 | tf_op args[5]
  2.4 1.5 %copy.27.wo_ref = bf16[896,448]{1,0:T(8,128)(2,1)} copy(bf16[896,448]{0,1:T(8,128)(2,1)S(1)} %copy-done.4) | data formatting | bytes 1605632 | tf_op args[6]
  3.9 0.8 copy.72
  4.7 0.8 copy.25.mem_ref
  5.7 0.6 pad.4.nb_ref
  6.3 69.6 %shard_map.91 = (bf16[2,2,64,896]{3,2,1,0:T(8,128)(2,1)}, bf16[128,896]{1,0:T(8,128)(2,1)}, bf16[896,448]{1,0:T(8,128)(2,1)}, bf16[896,448]{1,0:T(8,128)(2,1)}, bf16[8,2,896,128]{3,2,1,0:T(8,128)(2,1)}) custom-call(s32[8,128]{1,0:T(8,128)} %pad.4.nb_ref, bf16[8,2,64,896]{3,2,1,0:T(8,128)(2,1)} %bitcast.77, bf16[128,896]{1,0:T(8,128)(2,1)} %copy.25.mem_ref, ...), custom_call_target="tpu_custom_call" | custom-call | tf_op jit(solution)/shard_map/pallas_call | solution.py:270
  75.8 1.2 multiply_reduce_fusion.1
  77.1 1.2 fusion.26
  78.3 2.0 %fusion.15 = bf16[256,896]{1,0:T(8,128)(2,1)S(1)} fusion(bf16[256,896]{1,0:T(8,128)(2,1)S(1)} %fusion.26, bf16[896,448]{1,0:T(8,128)(2,1)} %get-tuple-element.13, bf16[896,448]{1,0:T(8,128)(2,1)S(1)} %copy-done.1), kind=kOutput, calls=%fused_computation.17 | convolution fusion | flops 414482432 | bytes 2523136 | tf_op jit(solution)/shard_map/dot_general | solution.py:285
  80.3 0.7 reshape.84
  81.6 1.0 fusion.38
  83.1 0.7 convolution_multiply_fusion.1
  84.4 0.5 copy.34
  85.3 2.5 %multiply_reduce_fusion = (f32[256]{0:T(256)S(1)}, f32[256,896]{1,0:T(8,128)S(1)}) fusion(bf16[896,448]{1,0:T(8,128)(2,1)} %get-tuple-element.14, bf16[896,448]{1,0:T(8,128)(2,1)S(1)} %copy-done, bf16[112,8,2,128]{3,2,1,0:T(2,128)(2,1)S(1)} %bitcast.84, bf16[256,896]{1,0:T(8,128)(2,1)S(1)} %bitcast.78), kind=kOutput, calls=%fused_computation.32 | convolution fusion | flops 415170304 | bytes 3441664 | tf_op jit(solution)/shard_map/dot_general | solution.py:295
  87.9 6.0 %all-gather = bf16[512,896]{1,0:T(8,128)(2,1)S(1)} all-gather(bf16[256,896]{1,0:T(8,128)(2,1)S(1)} %multiply_convert_fusion), channel_id=2, replica_groups=mesh['groups'=2,'span'=8,'head'=2] {'head'}, dimensions={0}, use_global_device_ids=true | all-gather | bytes 1376256 | tf_op jit(solution)/shard_map/all_gather | solution.py:352
  93.9 3.8 %convert_bitcast_fusion = bf16[512,2,8,128]{0,3,1,2:T(8,128)(2,1)} fusion(bf16[8,2,896,128]{3,2,1,0:T(8,128)(2,1)S(1)} %copy-done.8, bf16[512,896]{1,0:T(8,128)(2,1)S(1)} %all-gather), kind=kOutput, calls=%fused_computation.1 | convolution fusion | flops 1880096768 | bytes 6684672 | tf_op jit(solution)/shard_map/re,nsec->rsnc/dot_general | solution.py:354
  97.7 2.5 %reshape.75 = bf16[2,2,128,2,8,128]{2,1,0,5,3,4:T(2,128)(2,1)S(1)} reshape(bf16[512,2,8,128]{0,3,1,2:T(8,128)(2,1)} %convert_bitcast_fusion) | data formatting | bytes 4194304 | tf_op jit(solution)/shard_map/reshape | solution.py:358
  100.3 2.3 %fusion.37 = (bf16[2,2,128,1,8,128]{2,1,0,5,3,4:T(2,128)(2,1)}, bf16[2,2,128,1,8,128]{2,1,0,5,3,4:T(2,128)(2,1)S(1)}) fusion(bf16[2,2,128,2,8,128]{2,1,0,5,3,4:T(2,128)(2,1)S(1)} %reshape.75), kind=kLoop, calls=%fused_computation.52 | loop fusion | bytes 4194304 | tf_op jit(solution)/shard_map/slice | solution.py:361
  102.6 2.6 %copy.51 = bf16[2,2,128,1,8,128]{5,2,0,4,1,3:T(8,128)(2,1)S(1)} copy(bf16[2,2,128,1,8,128]{2,1,0,5,3,4:T(2,128)(2,1)} %get-tuple-element.15) | data formatting | bytes 2097152
  105.2 0.6 fusion.40
  106.2 0.9 copy.52
  107.7 0.8 copy.73
  108.5 41.1 %shard_map.92 = bf16[128,2048]{1,0:T(8,128)(2,1)} custom-call(bf16[128,1024]{1,0:T(8,128)(2,1)} %bitcast.79, bf16[1024,512]{1,0:T(8,128)(2,1)} %w_ref.1, bf16[128,2048]{1,0:T(8,128)(2,1)} %states_ref.1), custom_call_target="tpu_custom_call" | custom-call | tf_op jit(solution)/shard_map/pallas_call | solution.py:270
  149.6 1.9 %copy.75 = bf16[128,2048]{1,0:T(8,128)(2,1)} copy(bf16[128,2048]{1,0:T(8,128)(2,1)} %shard_map.92) | data formatting | bytes 1048576
  (36 shorter events, 3.5 us)
Async XLA Ops:
  0.0 2.4 %copy-start.4 = (bf16[896,448]{0,1:T(8,128)(2,1)S(1)}, bf16[896,448]{0,1:T(8,128)(2,1)}, u32[]{:S(2)}) copy-start(bf16[896,448]{0,1:T(8,128)(2,1)} %param.15) | copy-start | bytes 2408452
  0.0 3.9 %copy-start.5 = (bf16[896,2,128]{2,1,0:T(2,128)(2,1)S(1)}, bf16[896,2,128]{2,1,0:T(2,128)(2,1)}, u32[]{:S(2)}) copy-start(bf16[896,2,128]{2,1,0:T(2,128)(2,1)} %param.16) | copy-start | bytes 1376260
  0.0 4.7 %copy-start.3 = (bf16[128,2,448]{0,2,1:T(8,128)(2,1)S(1)}, bf16[128,2,448]{0,2,1:T(8,128)(2,1)}, u32[]{:S(2)}) copy-start(bf16[128,2,448]{0,2,1:T(8,128)(2,1)} %param.11) | copy-start | bytes 688132
  0.0 5.6 %copy-start.9 = (s32[2,2]{1,0:T(2,128)S(1)}, s32[2,2]{1,0:T(2,128)}, u32[]{:S(2)}) copy-start(s32[2,2]{1,0:T(2,128)} %param.13) | copy-start | bytes 52
  6.3 72.0 %copy-start.1 = (bf16[896,448]{1,0:T(8,128)(2,1)S(1)}, bf16[896,448]{1,0:T(8,128)(2,1)}, u32[]{:S(2)}) copy-start(bf16[896,448]{1,0:T(8,128)(2,1)} %copy.26.wq_ref) | copy-start | bytes 2408452
  78.3 2.7 %copy-start.7 = (bf16[128,896]{1,0:T(8,128)(2,1)S(1)}, bf16[128,896]{1,0:T(8,128)(2,1)}, u32[]{:S(2)}) copy-start(bf16[128,896]{1,0:T(8,128)(2,1)} %get-tuple-element.12) | copy-start | bytes 688132
  84.0 1.2 copy-start
  84.0 1.3 copy-start.2
  85.3 8.6 %copy-start.8 = (bf16[8,2,896,128]{3,2,1,0:T(8,128)(2,1)S(1)}, bf16[8,2,896,128]{3,2,1,0:T(8,128)(2,1)}, u32[]{:S(2)}) copy-start(bf16[8,2,896,128]{3,2,1,0:T(8,128)(2,1)} %get-tuple-element.10) | copy-start | bytes 11010052
  102.5 2.6 %copy-start.6 = (bf16[128,1024]{1,0:T(8,128)(2,1)S(1)}, bf16[128,1024]{1,0:T(8,128)(2,1)}, u32[]{:S(2)}) copy-start(bf16[128,1024]{1,0:T(8,128)(2,1)} %param.10) | copy-start | bytes 786436

commit v2 on v1

--- a/solution.py
+++ b/solution.py
@@ -49,26 +49,28 @@
 
 
 class Ring:
-    def __init__(self, n, own, out, halves, sems):
+    def __init__(self, n, own, slot, halves, sems):
         me = lax.axis_index("span")
-        self.n, self.own, self.out, self.halves, self.sems = n, own, out, halves, sems
+        self.n, self.own, self.slot, self.halves, self.sems = n, own, slot, halves, sems
         self.place = ring_place(me, n)
         self.right = ring_span((self.place + 1) % n, n)
         self.left = ring_span((self.place + n - 1) % n, n)
         self.steps = n // 2
         self.copies = []
 
+    def cut(self, ref, t, side):
+        return self.halves(ref, side) if t == self.steps - 1 else ref
+
     def start(self, t):
         n = self.n
         pair = []
         for side, target in ((0, self.right), (1, self.left)):
-            place = (self.place + (n - t if side == 0 else t)) % n
-            block = ring_span(place, n)
-            src = self.own if t == 0 else self.out.at[block]
-            dst = self.out.at[block]
-            if t == self.steps - 1:
-                src, dst = self.halves(src, side), self.halves(dst, side)
-            copy = remote(src, dst, self.sems.at[0, side, t], self.sems.at[1, side, t], span=target)
+            block = ring_span((self.place + (n - t if side == 0 else t)) % n, n)
+            src = self.own if t == 0 else self.slot(block)
+            copy = remote(
+                self.cut(src, t, side), self.cut(self.slot(block), t, side),
+                self.sems.at[0, side, t], self.sems.at[1, side, t], span=target,
+            )
             copy.start()
             pair.append(copy)
         self.copies.append(pair)
@@ -77,8 +79,7 @@
         for copy in self.copies[t]:
             copy.wait_recv()
         n = self.n
-        blocks = [ring_span((self.place + n - t - 1) % n, n), ring_span((self.place + t + 1) % n, n)]
-        return blocks[:1] if t == self.steps - 1 else blocks
+        return [ring_span((self.place + n - t - 1) % n, n), ring_span((self.place + t + 1) % n, n)]
 
     def finish(self):
         for pair in self.copies:
@@ -86,19 +87,47 @@
                 copy.wait_send()
 
 
+def weigh(scores, mask):
+    scores = jnp.where(mask, scores, -jnp.inf)
+    raised = jnp.exp(scores - jnp.max(scores, axis=-1, keepdims=True))
+    return (raised * (1.0 / jnp.sum(raised, axis=-1, keepdims=True))).astype(jnp.bfloat16)
+
+
+def same_span(shape, rows_each, lanes_each, spans):
+    row = lax.broadcasted_iota(jnp.int32, shape, 0) // rows_each
+    lane = (lax.broadcasted_iota(jnp.int32, shape, 1) // lanes_each) % spans
+    return row == lane
+
+
+def dot(a, b, dims=((1,), (0,))):
+    return lax.dot_general(a, b, (dims, ((), ())), preferred_element_type=jnp.float32)
+
+
 def fetch_kernel(
-    n, spans, nb_ref, pas_ref, mem_ref, wq_ref, wo_ref, kv_ref,
-    cop_ref, memo_ref, wqo_ref, woo_ref, kvg_ref,
-    nbg, nbs, picks, got, swap, local_sem, nb_sem, pas_sem, swap_sem, w_sem, ring_sem,
+    n, groups, spans, fused, nb_ref, pas_ref, mem_ref, wq_ref, wo_ref, kv_ref, ask_ref, *rest,
 ):
+    if fused:
+        att_ref, enc, kvg = rest[:3]
+    else:
+        enc, kvg = rest[:2]
+    (
+        nbg, nbs, picks, got, swap, cop, mem, wq, wo, query, mixed,
+        local_sem, nb_sem, pas_sem, swap_sem, w_sem, enc_sem, ring_sem, twin_sem,
+    ) = rest[3 if fused else 2:]
     me = lax.axis_index("span")
     head = lax.axis_index("head")
+    group = lax.axis_index("groups")
     other = 1 - head
+    twin = group + 1 - 2 * (group % 2)
+    part = group % 2
+    half_rows = PT // 2
+    half_e = wq_ref.shape[0]
     barrier = pltpu.get_barrier_semaphore()
     for d in range(1, n):
         pl.semaphore_signal(barrier, inc=1, device_id={"span": (me + d) % n}, device_id_type=MESH)
     pl.semaphore_signal(barrier, inc=1, device_id={"head": other}, device_id_type=MESH)
-    pl.semaphore_wait(barrier, n)
+    pl.semaphore_signal(barrier, inc=1, device_id={"groups": twin}, device_id_type=MESH)
+    pl.semaphore_wait(barrier, n + 1)
 
     nb_copies = []
     for d in range(1, n):
@@ -107,14 +136,17 @@
         nb_copies.append(copy)
     own_nb = pltpu.make_async_copy(nb_ref, nbg.at[me], local_sem.at[0])
     own_nb.start()
-    w_copies = [
-        remote(src, dst, w_sem.at[0, i], w_sem.at[1, i], head=other)
-        for i, (src, dst) in enumerate(((mem_ref, memo_ref), (wq_ref, wqo_ref), (wo_ref, woo_ref)))
-    ]
-    for copy in w_copies:
-        copy.start()
-    own_kv = pltpu.make_async_copy(kv_ref, kvg_ref.at[me], local_sem.at[1])
-    own_kv.start()
+    mine = pl.ds(pl.multiple_of(head * half_e, half_e), half_e)
+    w_copies, own_copies = [], []
+    for i, (src, dst) in enumerate((
+        (mem_ref.at[0], mem.at[0, mine]), (mem_ref.at[1], mem.at[1, mine]), (wq_ref, wq.at[mine]), (wo_ref, wo.at[mine]),
+    )):
+        w_copies.append(remote(src, dst, w_sem.at[0, i], w_sem.at[1, i], head=other))
+        w_copies[-1].start()
+        own_copies.append(pltpu.make_async_copy(src, dst, local_sem.at[3 + i]))
+        own_copies[-1].start()
+    own_copies.append(pltpu.make_async_copy(kv_ref, kvg.at[me], local_sem.at[1]))
+    own_copies[-1].start()
     own_nb.wait()
     for copy in nb_copies:
         copy.wait()
@@ -140,7 +172,24 @@
         copy.start()
         pas_copies.append(copy)
 
-    ring = Ring(n, kv_ref, kvg_ref, lambda ref, side: ref.at[side], ring_sem)
+    cut_rows = kv_ref.shape[1] // 2
+    ring = Ring(
+        n, kv_ref.at[part], lambda block: kvg.at[block, part],
+        lambda ref, side: ref.at[pl.ds(side * cut_rows, cut_rows)], ring_sem,
+    )
+    twins = []
+
+    def pass_on(t):
+        blocks = ring.arrived(t)
+        if t + 1 < ring.steps:
+            ring.start(t + 1)
+        for side, block in enumerate(blocks):
+            piece = ring.cut(ring.slot(block), t, side)
+            copy = remote(piece, piece, twin_sem.at[0, side, t], twin_sem.at[1, side, t], groups=twin)
+            copy.start()
+            twins.append(copy)
+        return blocks
+
     ring.start(0)
     for copy in pas_copies:
         copy.wait_recv()
@@ -148,18 +197,71 @@
     for c in range(spans):
         swap[c] = got[nbs[me, 0, c * NB + other] // PS_DEV]
     for c in range(spans):
-        cop_ref[c, head] = got[nbs[me, 0, c * NB + head] // PS_DEV]
-        copy = remote(swap.at[c], cop_ref.at[c, head], swap_sem.at[0, c], swap_sem.at[1, c], head=other)
+        spot = cop.at[pl.ds(pl.multiple_of(c * PT + head * half_rows, half_rows), half_rows)]
+        copy = remote(swap.at[c], spot, swap_sem.at[0, c], swap_sem.at[1, c], head=other)
         copy.start()
         swaps.append(copy)
+        spot[...] = got[nbs[me, 0, c * NB + head] // PS_DEV]
+    for copy in own_copies:
+        copy.wait()
+    for copy in w_copies:
+        copy.wait()
+    for copy in swaps:
+        copy.wait()
+
+    rows = cop.shape[0]
+    tokens = mem.shape[2]
+    width = cop.shape[1]
+    values = cop[...].astype(jnp.float32)
+    query[...] = dot(rms_rows(values).astype(jnp.bfloat16), wq[...], ((1,), (1,))).astype(jnp.bfloat16)
+    mask = same_span((rows, tokens), PT, CT, spans)
+    feature = lax.broadcasted_iota(jnp.int32, (2 * EHD, tokens), 0) // EHD
+    for j in range(width // (2 * EHD)):
+        lines = pl.ds(j * 2 * EHD, 2 * EHD)
+        total = None
+        for e in range(2):
+            keys = jnp.where(feature == e, mem[0, lines], jnp.bfloat16(0))
+            vals = jnp.where(feature == e, mem[1, lines], jnp.bfloat16(0))
+            scores = dot(query[:, lines], keys) * (1.0 / math.sqrt(EHD))
+            term = dot(weigh(scores, mask), vals, ((1,), (1,)))
+            total = term if e == 0 else total + term
+        mixed[:, lines] = total.astype(jnp.bfloat16)
+    arrivals = [pass_on(0)]
+    branch = dot(mixed[...], wo[...])
+    enc[head] = rms_rows(cop[...].astype(jnp.float32) + branch).astype(jnp.bfloat16)
+    enc_copy = remote(enc.at[head], enc.at[head], enc_sem.at[0], enc_sem.at[1], head=other)
+    enc_copy.start()
+    arrivals.append(pass_on(1))
+    enc_copy.wait_recv()
+
+    if fused:
+        asks = ask_ref.shape[0]
+        dec_mask = same_span((asks, NB * rows), CT, PT, spans)
+
+        def attend(block):
+            for m in range(kv_ref.shape[2] // HD):
+                flat = enc[...].reshape(NB * rows, width)
+                lanes = pl.ds(m * HD, HD)
+                keys = dot(flat, kvg[block, 0, :, lanes]).astype(jnp.bfloat16)
+                vals = dot(flat, kvg[block, 1, :, lanes]).astype(jnp.bfloat16)
+                spot = pl.ds(pl.multiple_of(block * kv_ref.shape[2] + m * HD, HD), HD)
+                scores = dot(ask_ref[:, spot], keys, ((1,), (1,))) * (1.0 / math.sqrt(HD))
+                att_ref[:, spot] = dot(weigh(scores, dec_mask), vals).astype(jnp.bfloat16)
+
+        attend(me)
+
     for t in range(ring.steps):
-        ring.arrived(t)
-        if t + 1 < ring.steps:
-            ring.start(t + 1)
-    own_kv.wait()
-    for copy in swaps + w_copies:
-        copy.wait()
-    for copy in pas_copies:
+        if t >= len(arrivals):
+            arrivals.append(pass_on(t))
+        for copy in twins[2 * t:2 * t + 2]:
+            copy.wait_recv()
+        if t + 1 < ring.steps and t + 1 >= len(arrivals):
+            arrivals.append(pass_on(t + 1))
+        if fused:
+            for block in arrivals[t][:1 if t == ring.steps - 1 else 2]:
+                attend(block)
+    enc_copy.wait_send()
+    for copy in pas_copies + twins:
         copy.wait_send()
     ring.finish()
 
@@ -187,7 +289,10 @@
                 )
     pl.semaphore_wait(barrier, 2 * n - 1)
 
-    ring = Ring(n, att_ref, gathered, lambda ref, side: ref.at[pl.ds(side * half_rows, half_rows)], ring_sem)
+    ring = Ring(
+        n, att_ref, lambda block: gathered.at[block],
+        lambda ref, side: ref.at[pl.ds(side * half_rows, half_rows)], ring_sem,
+    )
     ring.start(0)
     crossings, returns = [], []
 
@@ -231,7 +336,7 @@
         blocks = ring.arrived(t)
         if t + 1 < ring.steps:
             ring.start(t + 1)
-        for block in blocks:
+        for block in blocks[:1 if t == ring.steps - 1 else 2]:
             project(block, gathered.at[block])
             send_across()
             give_back()
@@ -277,25 +382,23 @@
     )(*operands)
 
 
-def encode_branch(copies, memory, query_w, out_w):
-    span_count = copies.shape[0]
-    head_count = memory.shape[3]
-    flat_rows = copies.reshape(-1, E).astype(jnp.float32)
-    normed = rms_rows(flat_rows).astype(jnp.bfloat16)
-    enc_query = jnp.dot(normed, query_w, preferred_element_type=jnp.float32).astype(jnp.bfloat16)
-    enc_query = enc_query.reshape(span_count, PT, head_count, EHD)
+def decode(encoded, kv_all, span_queries, span_count):
+    dec_kv = jnp.einsum(
+        "re,nsec->rsnc", encoded.reshape(-1, E), kv_all, preferred_element_type=jnp.float32
+    ).astype(jnp.bfloat16)
+    head_count = span_queries.shape[1] // HD
+    dec_kv = dec_kv.reshape(NB, span_count, PT, 2, head_count, HD)
+    dec_query = span_queries.reshape(span_count, CT, head_count, HD)
     scores = jnp.einsum(
-        "cqhd,ckhd->chqk", enc_query, memory[:, :, 0], preferred_element_type=jnp.float32
-    ) / math.sqrt(EHD)
+        "cqhd,ncphd->chqnp", dec_query, dec_kv[:, :, :, 0], preferred_element_type=jnp.float32
+    ) / math.sqrt(HD)
+    scores = scores.reshape(span_count, head_count, CT, NB * PT)
     weights = softmax_rows(scores).astype(jnp.bfloat16)
-    mixed_heads = jnp.einsum(
-        "chqk,ckhd->cqhd", weights, memory[:, :, 1], preferred_element_type=jnp.float32
-    )
-    mixed_heads = mixed_heads.astype(jnp.bfloat16).reshape(-1, head_count * EHD)
-    branch = lax.dot_general(
-        mixed_heads, out_w, (((1,), (1,)), ((), ())), preferred_element_type=jnp.float32
-    )
-    return (flat_rows, branch)
+    weights = weights.reshape(span_count, head_count, CT, NB, PT)
+    attended = jnp.einsum(
+        "chqnp,ncphd->cqhd", weights, dec_kv[:, :, :, 1], preferred_element_type=jnp.float32
+    )
+    return attended.astype(jnp.bfloat16).reshape(span_count * CT, head_count * HD)
 
 
 def body(
@@ -317,56 +420,39 @@
     flat_nb = neighbours.reshape(1, -1)
     nb = jnp.pad(flat_nb, ((0, 7), (0, 128 - flat_nb.shape[1])))
     kv = kv_weight.transpose(1, 0, 2)
-    memory_flat = span_memory.reshape(span_memory.shape[0], -1)
+    memory = span_memory.transpose(1, 2, 0)
+    rows, tokens = span_count * PT, span_memory.shape[0]
     sds = jax.ShapeDtypeStruct
-    copies, memory_other, query_other, out_other, kv_all = vmem_call(
-        functools.partial(fetch_kernel, n, span_count), 0,
-        [
-            sds((span_count, 2, half_rows, E), bf16),
-            sds(memory_flat.shape, bf16),
-            sds(enc_query_w.shape, bf16),
-            sds(enc_out_w.shape, bf16),
-            sds((n,) + kv.shape, bf16),
-        ],
-        [
+    fused = kv.shape[2] % HD == 0
+    enc_shape, kv_shape = (NB, rows, E), (n,) + kv.shape
+    found = vmem_call(
+        functools.partial(fetch_kernel, n, lax.axis_size("groups"), span_count, fused), 0,
+        [sds(span_queries.shape, bf16)] if fused else [sds(enc_shape, bf16), sds(kv_shape, bf16)],
+        ([pltpu.VMEM(enc_shape, bf16), pltpu.VMEM(kv_shape, bf16)] if fused else []) + [
             pltpu.VMEM((n, 8, 128), jnp.int32),
             pltpu.SMEM((n, 8, 128), jnp.int32),
             pltpu.VMEM((n, half_rows, E), bf16),
             pltpu.VMEM((n, half_rows, E), bf16),
             pltpu.VMEM((span_count, half_rows, E), bf16),
-            dma((3,)),
+            pltpu.VMEM((rows, E), bf16),
+            pltpu.VMEM((2, E, tokens), bf16),
+            pltpu.VMEM((E, E), bf16),
+            pltpu.VMEM((E, E), bf16),
+            pltpu.VMEM((rows, E), bf16),
+            pltpu.VMEM((rows, E), bf16),
+            dma((7,)),
             dma((2, n)),
             dma((2, n)),
             dma((2, span_count)),
-            dma((2, 3)),
+            dma((2, 4)),
+            dma((2,)),
+            dma((2, 2, n // 2)),
             dma((2, 2, n // 2)),
         ],
-        nb, passages.reshape(-1, 2, half_rows, E), memory_flat, enc_query_w, enc_out_w, kv,
-    )
-    query_full = jnp.concatenate([enc_query_w, query_other], axis=1)
-    out_full = jnp.concatenate([enc_out_w, out_other], axis=1)
-    memory = jnp.concatenate([span_memory, memory_other.reshape(span_memory.shape)], axis=2)
-    memory = memory.reshape(span_count, CT, 2, -1, EHD)
-    own_rows, own_branch = encode_branch(copies, memory, query_full, out_full)
-    encoded = rms_rows(own_rows + own_branch).astype(bf16)
-    all_encoded = lax.all_gather(encoded[None], "head", axis=0, tiled=True)
-    flat_encoded = all_encoded.reshape(-1, E)
-    dec_kv = jnp.einsum(
-        "re,nsec->rsnc", flat_encoded, kv_all, preferred_element_type=jnp.float32
-    ).astype(bf16)
-    head_count = span_queries.shape[1] // HD
-    dec_kv = dec_kv.reshape(NB, span_count, PT, 2, head_count, HD)
-    dec_query = span_queries.reshape(span_count, CT, head_count, HD)
-    scores = jnp.einsum(
-        "cqhd,ncphd->chqnp", dec_query, dec_kv[:, :, :, 0], preferred_element_type=jnp.float32
-    ) / math.sqrt(HD)
-    scores = scores.reshape(span_count, head_count, CT, NB * PT)
-    weights = softmax_rows(scores).astype(bf16).reshape(span_count, head_count, CT, NB, PT)
-    attended = jnp.einsum(
-        "chqnp,ncphd->cqhd", weights, dec_kv[:, :, :, 1], preferred_element_type=jnp.float32
-    )
-    attended = attended.astype(bf16).reshape(span_count * CT, head_count * HD)
-    rows, width = attended.shape[0], out_weight.shape[1]
+        nb, passages.reshape(-1, 2, half_rows, E), memory, enc_query_w.T, enc_out_w.T, kv, span_queries,
+    )
+    attended = found[0] if fused else decode(found[0], found[1], span_queries, span_count)
+    rows, width = tokens, out_weight.shape[1]
     return vmem_call(
         functools.partial(out_kernel, n), 1,
         sds(span_states.shape, bf16),

time: 152 us -> 126 us (0.83)
  local copies, waits for them, and re-layouts: 21.1 us -> 5.08 us
  matrix products: 10.3 us -> 0 us
  Pallas kernels: 111 us -> 121 us
  blocking collectives: 6.02 us -> 0 us
  other arithmetic: 3.14 us -> 0 us
    dot_general x7 -> x0, matrix products: 10.3 us -> none  [the longest x1 3.77 us: body(): jnp.einsum('re,nsec->rsnc', flat_encoded, kv_all, preferred_element_type=...]
    pallas_call x2, Pallas kernels: 111 us -> 121 us  [vmem_call(): pl.pallas_call(kernel, out_shape=out_shape, in_specs=[pl.BlockSpec(memory...]
    unnamed x29 -> x2, local copies, waits for them, and re-layouts: 11.7 us -> 3.73 us
    all_gather x1 -> x0, blocking collectives: 6.02 us -> none  [body(): all_encoded = lax.all_gather(encoded[None], 'head', axis=0, tiled=True)]
    reshape x5 -> x0, local copies, waits for them, and re-layouts: 4.47 us -> none  [the longest x1 2.55 us: body(): dec_kv = dec_kv.reshape(NB, span_count, PT, 2, head_count, HD)]
    slice x2 -> x0, local copies, waits for them, and re-layouts: 3.28 us -> none  [the longest x1 2.29 us: body(): dec_kv[:, :, :, 0]]
    reduce_sum x2 -> x0, other arithmetic: 1.59 us -> none  [the longest x1 1.19 us: rms_rows(): jnp.mean(values * values, axis=-1, keepdims=True) + epsilon]
where the time goes in v2:
time: 126 us
  Pallas kernels  121 us (96%)
  local copies, waits for them, and re-layouts  5.08 us (4%)
    pallas_call x2, Pallas kernels, vmem_call(): pl.pallas_call(kernel, out_shape=out_shape, in_specs=[pl.BlockSpec(memory...  121 us
    unnamed x2, local copies, waits for them, and re-layouts  3.73 us

profile of v2, /device:TPU:1, one launch (start us, length us, event | category | flops | bytes accessed | tf_op | source)
XLA Modules:
  0.0 125.7 jit_solution(16380862138973735681)
XLA Ops:
  0.0 0.8 reshape.6
  0.8 0.6 pad.4.nb_ref
  1.4 1.8 %copy.12 = bf16[896,2,128]{2,0,1:T(8,128)(2,1)} copy(bf16[896,2,128]{2,1,0:T(2,128)(2,1)} %param.16) | data formatting | bytes 917504 | tf_op args[7]
  3.2 68.6 %shard_map.91.att_ref = bf16[128,1024]{1,0:T(8,128)(2,1)} custom-call(s32[8,128]{1,0:T(8,128)} %pad.4.nb_ref, bf16[8,2,64,896]{3,2,1,0:T(8,128)(2,1)} %bitcast.7, bf16[2,448,128]{2,1,0:T(8,128)(2,1)} %bitcast.11, bf16[448,896]{1,0:T(8,128)(2,1)} %bitcast.9, bf16[448,896]{1,0:T(8,128)(2,1)} %bitcast.10, bf16[2,896,128]{2,1,0:T(8,128)(2,1)} %bitcast.8, ...), custom_call_target="tpu_custom_call" | custom-call | tf_op jit(solution)/shard_map/pallas_call | solution.py:375
  71.8 51.9 %shard_map.92 = bf16[128,2048]{1,0:T(8,128)(2,1)} custom-call(bf16[128,1024]{1,0:T(8,128)(2,1)} %shard_map.91.att_ref, bf16[1024,512]{1,0:T(8,128)(2,1)} %w_ref.1, bf16[128,2048]{1,0:T(8,128)(2,1)} %states_ref.1), custom_call_target="tpu_custom_call" | custom-call | tf_op jit(solution)/shard_map/pallas_call | solution.py:375
  123.8 1.9 %copy.14 = bf16[128,2048]{1,0:T(8,128)(2,1)} copy(bf16[128,2048]{1,0:T(8,128)(2,1)} %shard_map.92) | data formatting | bytes 1048576

commit v3 on v2

--- a/solution.py
+++ b/solution.py
@@ -49,42 +49,50 @@
 
 
 class Ring:
-    def __init__(self, n, own, slot, halves, sems):
+    def __init__(self, n, own, slots, sems):
         me = lax.axis_index("span")
-        self.n, self.own, self.slot, self.halves, self.sems = n, own, slot, halves, sems
+        self.n, self.own, self.slots, self.sems = n, own, slots, sems
         self.place = ring_place(me, n)
-        self.right = ring_span((self.place + 1) % n, n)
-        self.left = ring_span((self.place + n - 1) % n, n)
+        self.targets = (ring_span((self.place + 1) % n, n), ring_span((self.place + n - 1) % n, n))
         self.steps = n // 2
-        self.copies = []
-
-    def cut(self, ref, t, side):
-        return self.halves(ref, side) if t == self.steps - 1 else ref
-
-    def start(self, t):
+        self.copies = {}
+
+    def travels(self, t, side, k):
+        return t < self.steps - 1 or k % 2 == side
+
+    def block(self, t, side):
         n = self.n
-        pair = []
-        for side, target in ((0, self.right), (1, self.left)):
-            block = ring_span((self.place + (n - t if side == 0 else t)) % n, n)
-            src = self.own if t == 0 else self.slot(block)
-            copy = remote(
-                self.cut(src, t, side), self.cut(self.slot(block), t, side),
-                self.sems.at[0, side, t], self.sems.at[1, side, t], span=target,
-            )
-            copy.start()
-            pair.append(copy)
-        self.copies.append(pair)
-
-    def arrived(self, t):
-        for copy in self.copies[t]:
-            copy.wait_recv()
-        n = self.n
-        return [ring_span((self.place + n - t - 1) % n, n), ring_span((self.place + t + 1) % n, n)]
+        return ring_span((self.place + (n - t if side == 0 else t)) % n, n)
+
+    def send(self, t, side, k):
+        dst = self.slots(self.block(t, side))[k]
+        copy = remote(
+            self.own[k] if t == 0 else dst, dst,
+            self.sems.at[0, side, t, k], self.sems.at[1, side, t, k], span=self.targets[side],
+        )
+        copy.start()
+        self.copies[t, side, k] = copy
+
+    def start(self):
+        for k in range(len(self.own)):
+            for side in range(2):
+                if self.travels(0, side, k):
+                    self.send(0, side, k)
+
+    def advance(self, t, forward=None):
+        for k in range(len(self.own)):
+            for side in range(2):
+                if self.travels(t, side, k):
+                    self.copies[t, side, k].wait_recv()
+                    if t + 1 < self.steps and self.travels(t + 1, side, k):
+                        self.send(t + 1, side, k)
+                    if forward is not None:
+                        forward(t, side, k, self.block(t + 1, side))
+        return [self.block(t + 1, side) for side in range(1 if t == self.steps - 1 else 2)]
 
     def finish(self):
-        for pair in self.copies:
-            for copy in pair:
-                copy.wait_send()
+        for copy in self.copies.values():
+            copy.wait_send()
 
 
 def weigh(scores, mask):
@@ -103,17 +111,33 @@
     return lax.dot_general(a, b, (dims, ((), ())), preferred_element_type=jnp.float32)
 
 
+def greet_all(n):
+    me = lax.axis_index("span")
+    head = lax.axis_index("head")
+    barrier = pltpu.get_barrier_semaphore()
+    for d in range(n):
+        for hop in range(2):
+            if d or hop:
+                pl.semaphore_signal(
+                    barrier, inc=1,
+                    device_id={"span": (me + d) % n, "head": (head + hop) % 2}, device_id_type=MESH,
+                )
+    return barrier, 2 * n - 1
+
+
 def fetch_kernel(
-    n, groups, spans, fused, nb_ref, pas_ref, mem_ref, wq_ref, wo_ref, kv_ref, ask_ref, *rest,
+    n, groups, spans, fused, nb_ref, pas_in, mem_ref, wq_ref, wo_ref, kv_ref, ask_in, w_in, states_in, *rest,
 ):
     if fused:
-        att_ref, enc, kvg = rest[:3]
+        (out_ref, enc, kvg, att_ref, *tail) = rest[:4 + 11]
+        scratch = rest[4 + 11:]
     else:
         enc, kvg = rest[:2]
+        scratch = rest[2:]
     (
-        nbg, nbs, picks, got, swap, cop, mem, wq, wo, query, mixed,
+        pas_ref, ask_ref, nb_own, nbg, nbs, picks, got, swap, cop, mem, wq, wo, query, mixed,
         local_sem, nb_sem, pas_sem, swap_sem, w_sem, enc_sem, ring_sem, twin_sem,
-    ) = rest[3 if fused else 2:]
+    ) = scratch
     me = lax.axis_index("span")
     head = lax.axis_index("head")
     group = lax.axis_index("groups")
@@ -122,20 +146,51 @@
     part = group % 2
     half_rows = PT // 2
     half_e = wq_ref.shape[0]
-    barrier = pltpu.get_barrier_semaphore()
-    for d in range(1, n):
-        pl.semaphore_signal(barrier, inc=1, device_id={"span": (me + d) % n}, device_id_type=MESH)
-    pl.semaphore_signal(barrier, inc=1, device_id={"head": other}, device_id_type=MESH)
+    barrier, greeted = greet_all(n)
     pl.semaphore_signal(barrier, inc=1, device_id={"groups": twin}, device_id_type=MESH)
-    pl.semaphore_wait(barrier, n + 1)
+    loads = [pltpu.make_async_copy(pas_in, pas_ref, local_sem.at[7])]
+    if fused:
+        loads += [
+            pltpu.make_async_copy(ask_in, ask_ref, local_sem.at[8]),
+            pltpu.make_async_copy(w_in, tail[0], local_sem.at[9]),
+            pltpu.make_async_copy(states_in, tail[1], local_sem.at[10]),
+        ]
+    for copy in loads:
+        copy.start()
+    nb_own[...] = jnp.zeros_like(nb_own)
+    nb_own[:spans, :NB] = nb_ref[...]
+    pl.semaphore_wait(barrier, greeted + 1)
 
     nb_copies = []
     for d in range(1, n):
-        copy = remote(nb_ref, nbg.at[me], nb_sem.at[0, d], nb_sem.at[1, d], span=(me + d) % n)
+        copy = remote(nb_own, nbg.at[me], nb_sem.at[0, d], nb_sem.at[1, d], span=(me + d) % n)
         copy.start()
         nb_copies.append(copy)
-    own_nb = pltpu.make_async_copy(nb_ref, nbg.at[me], local_sem.at[0])
+    own_nb = pltpu.make_async_copy(nb_own, nbg.at[me], local_sem.at[0])
     own_nb.start()
+
+    depth = kv_ref.shape[1]
+    half, extra = depth // 2, depth // 4
+    near, far = part, 1 - part
+
+    def pieces(ref):
+        return [
+            ref.at[near, pl.ds(0, half)], ref.at[near, pl.ds(half, half)],
+            ref.at[far, pl.ds(0, extra // 2)], ref.at[far, pl.ds(extra // 2, extra // 2)],
+        ]
+
+    ring = Ring(n, pieces(kv_ref), lambda block: pieces(kvg.at[block]), ring_sem)
+    twins = [[] for _ in range(ring.steps)]
+
+    def to_twin(t, side, k, block):
+        if k < 2:
+            lines = pl.ds(extra, half - extra) if k == 0 else pl.ds(half, half)
+            piece = kvg.at[block, near, lines]
+            copy = remote(piece, piece, twin_sem.at[0, side, t, k], twin_sem.at[1, side, t, k], groups=twin)
+            copy.start()
+            twins[t].append(copy)
+
+    ring.start()
     mine = pl.ds(pl.multiple_of(head * half_e, half_e), half_e)
     w_copies, own_copies = [], []
     for i, (src, dst) in enumerate((
@@ -148,6 +203,7 @@
     own_copies.append(pltpu.make_async_copy(kv_ref, kvg.at[me], local_sem.at[1]))
     own_copies[-1].start()
     own_nb.wait()
+    loads[0].wait()
     for copy in nb_copies:
         copy.wait()
     to_scalar = pltpu.make_async_copy(nbg, nbs, local_sem.at[2])
@@ -157,7 +213,7 @@
     def pick(requester):
         index = jnp.int32(0)
         for e in range(spans * NB):
-            wanted = nbs[requester, 0, e]
+            wanted = nbs[requester, e // NB, e % NB]
             index = index + jnp.where(wanted // PS_DEV == me, wanted % PS_DEV, 0)
         return pas_ref[index, head]
 
@@ -172,36 +228,18 @@
         copy.start()
         pas_copies.append(copy)
 
-    cut_rows = kv_ref.shape[1] // 2
-    ring = Ring(
-        n, kv_ref.at[part], lambda block: kvg.at[block, part],
-        lambda ref, side: ref.at[pl.ds(side * cut_rows, cut_rows)], ring_sem,
-    )
-    twins = []
-
-    def pass_on(t):
-        blocks = ring.arrived(t)
-        if t + 1 < ring.steps:
-            ring.start(t + 1)
-        for side, block in enumerate(blocks):
-            piece = ring.cut(ring.slot(block), t, side)
-            copy = remote(piece, piece, twin_sem.at[0, side, t], twin_sem.at[1, side, t], groups=twin)
-            copy.start()
-            twins.append(copy)
-        return blocks
-
-    ring.start(0)
+    arrivals = [ring.advance(0, to_twin)]
     for copy in pas_copies:
         copy.wait_recv()
     swaps = []
     for c in range(spans):
-        swap[c] = got[nbs[me, 0, c * NB + other] // PS_DEV]
+        swap[c] = got[nbs[me, c, other] // PS_DEV]
     for c in range(spans):
         spot = cop.at[pl.ds(pl.multiple_of(c * PT + head * half_rows, half_rows), half_rows)]
         copy = remote(swap.at[c], spot, swap_sem.at[0, c], swap_sem.at[1, c], head=other)
         copy.start()
         swaps.append(copy)
-        spot[...] = got[nbs[me, 0, c * NB + head] // PS_DEV]
+        spot[...] = got[nbs[me, c, head] // PS_DEV]
     for copy in own_copies:
         copy.wait()
     for copy in w_copies:
@@ -226,15 +264,17 @@
             term = dot(weigh(scores, mask), vals, ((1,), (1,)))
             total = term if e == 0 else total + term
         mixed[:, lines] = total.astype(jnp.bfloat16)
-    arrivals = [pass_on(0)]
+    arrivals.append(ring.advance(1, to_twin))
     branch = dot(mixed[...], wo[...])
     enc[head] = rms_rows(cop[...].astype(jnp.float32) + branch).astype(jnp.bfloat16)
     enc_copy = remote(enc.at[head], enc.at[head], enc_sem.at[0], enc_sem.at[1], head=other)
     enc_copy.start()
-    arrivals.append(pass_on(1))
+    if ring.steps > 2:
+        arrivals.append(ring.advance(2, to_twin))
     enc_copy.wait_recv()
 
     if fused:
+        loads[1].wait()
         asks = ask_ref.shape[0]
         dec_mask = same_span((asks, NB * rows), CT, PT, spans)
 
@@ -252,23 +292,31 @@
 
     for t in range(ring.steps):
         if t >= len(arrivals):
-            arrivals.append(pass_on(t))
-        for copy in twins[2 * t:2 * t + 2]:
+            arrivals.append(ring.advance(t, to_twin))
+        for copy in twins[t]:
             copy.wait_recv()
-        if t + 1 < ring.steps and t + 1 >= len(arrivals):
-            arrivals.append(pass_on(t + 1))
         if fused:
-            for block in arrivals[t][:1 if t == ring.steps - 1 else 2]:
+            for block in arrivals[t]:
                 attend(block)
+    if fused:
+        loads[2].wait()
+        loads[3].wait()
+        out_stage(n, att_ref, tail[0], tail[1], out_ref, *tail[2:])
     enc_copy.wait_send()
-    for copy in pas_copies + twins:
+    for copy in pas_copies + [copy for pair in twins for copy in pair]:
         copy.wait_send()
     ring.finish()
 
 
-def out_kernel(
+def out_kernel(n, *refs):
+    barrier, greeted = greet_all(n)
+    pl.semaphore_wait(barrier, greeted)
+    out_stage(n, *refs)
+
+
+def out_stage(
     n, att_ref, w_ref, states_ref, out_ref,
-    gathered, part, crossed, summed, back, ring_sem, cross_sem, send_sem, back_sem, local_sem,
+    gathered, part, crossed, summed, back, ring_sem, cross_sem, send_sem, back_sem,
 ):
     me = lax.axis_index("span")
     head = lax.axis_index("head")
@@ -279,21 +327,12 @@
     rows = att_ref.shape[0]
     half_rows = rows // 2
     width = w_ref.shape[1]
-    barrier = pltpu.get_barrier_semaphore()
-    for d in range(n):
-        for hop in range(2):
-            if d or hop:
-                pl.semaphore_signal(
-                    barrier, inc=1,
-                    device_id={"span": (me + d) % n, "head": (head + hop) % 2}, device_id_type=MESH,
-                )
-    pl.semaphore_wait(barrier, 2 * n - 1)
-
-    ring = Ring(
-        n, att_ref, lambda block: gathered.at[block],
-        lambda ref, side: ref.at[pl.ds(side * half_rows, half_rows)], ring_sem,
-    )
-    ring.start(0)
+
+    def pieces(ref):
+        return [ref.at[pl.ds(k * half_rows, half_rows)] for k in range(2)]
+
+    ring = Ring(n, pieces(att_ref), lambda block: pieces(gathered.at[block]), ring_sem)
+    ring.start()
     crossings, returns = [], []
 
     def project(block, rows_ref):
@@ -333,10 +372,7 @@
     project(me, att_ref)
     send_across()
     for t in range(ring.steps):
-        blocks = ring.arrived(t)
-        if t + 1 < ring.steps:
-            ring.start(t + 1)
-        for block in blocks[:1 if t == ring.steps - 1 else 2]:
+        for block in ring.advance(t):
             project(block, gathered.at[block])
             send_across()
             give_back()
@@ -369,14 +405,12 @@
             copy.wait_send()
 
 
-def vmem_call(kernel, collective_id, out_shape, scratch_shapes, *operands):
-    outs = out_shape if isinstance(out_shape, (list, tuple)) else [out_shape]
-    specs = [pl.BlockSpec(memory_space=pltpu.VMEM)] * len(outs)
+def call(kernel, collective_id, out_shape, scratch_shapes, spaces, *operands):
     return pl.pallas_call(
         kernel,
         out_shape=out_shape,
-        in_specs=[pl.BlockSpec(memory_space=pltpu.VMEM)] * len(operands),
-        out_specs=specs if isinstance(out_shape, (list, tuple)) else specs[0],
+        in_specs=[pl.BlockSpec(memory_space=space) for space in spaces],
+        out_specs=[pl.BlockSpec(memory_space=pltpu.VMEM)] * len(out_shape),
         scratch_shapes=scratch_shapes,
         compiler_params=pltpu.CompilerParams(collective_id=collective_id, has_side_effects=True),
     )(*operands)
@@ -417,59 +451,67 @@
     bf16 = jnp.bfloat16
     dma = pltpu.SemaphoreType.DMA
     half_rows = PT // 2
-    flat_nb = neighbours.reshape(1, -1)
-    nb = jnp.pad(flat_nb, ((0, 7), (0, 128 - flat_nb.shape[1])))
     kv = kv_weight.transpose(1, 0, 2)
     memory = span_memory.transpose(1, 2, 0)
     rows, tokens = span_count * PT, span_memory.shape[0]
     sds = jax.ShapeDtypeStruct
     fused = kv.shape[2] % HD == 0
     enc_shape, kv_shape = (NB, rows, E), (n,) + kv.shape
-    found = vmem_call(
+    states, width = sds(span_states.shape, bf16), out_weight.shape[1]
+    out_scratch = [
+        pltpu.VMEM((n,) + span_queries.shape, bf16),
+        pltpu.VMEM((n, 2, tokens // 2, width), bf16),
+        pltpu.VMEM((n, tokens // 2, width), bf16),
+        pltpu.VMEM((n, tokens // 2, width), bf16),
+        pltpu.VMEM((n // 2, 2, tokens // 2, width), bf16),
+        dma((2, 2, n // 2, 2)),
+        dma((2, n)),
+        dma((n,)),
+        dma((n // 2, 2)),
+    ]
+    scratch = [
+        pltpu.VMEM((passages.shape[0] // PT, 2, half_rows, E), bf16),
+        pltpu.VMEM(span_queries.shape if fused else (16, 128), bf16),
+        pltpu.VMEM((8, 128), jnp.int32),
+        pltpu.VMEM((n, 8, 128), jnp.int32),
+        pltpu.SMEM((n, 8, 128), jnp.int32),
+        pltpu.VMEM((n, half_rows, E), bf16),
+        pltpu.VMEM((n, half_rows, E), bf16),
+        pltpu.VMEM((span_count, half_rows, E), bf16),
+        pltpu.VMEM((rows, E), bf16),
+        pltpu.VMEM((2, E, tokens), bf16),
+        pltpu.VMEM((E, E), bf16),
+        pltpu.VMEM((E, E), bf16),
+        pltpu.VMEM((rows, E), bf16),
+        pltpu.VMEM((rows, E), bf16),
+        dma((11,)),
+        dma((2, n)),
+        dma((2, n)),
+        dma((2, span_count)),
+        dma((2, 4)),
+        dma((2,)),
+        dma((2, 2, n // 2, 4)),
+        dma((2, 2, n // 2, 2)),
+    ]
+    if fused:
+        scratch = [
+            pltpu.VMEM(enc_shape, bf16), pltpu.VMEM(kv_shape, bf16), pltpu.VMEM(span_queries.shape, bf16),
+            pltpu.VMEM(out_weight.shape, bf16), pltpu.VMEM(span_states.shape, bf16),
+        ] + out_scratch + scratch
+    found = call(
         functools.partial(fetch_kernel, n, lax.axis_size("groups"), span_count, fused), 0,
-        [sds(span_queries.shape, bf16)] if fused else [sds(enc_shape, bf16), sds(kv_shape, bf16)],
-        ([pltpu.VMEM(enc_shape, bf16), pltpu.VMEM(kv_shape, bf16)] if fused else []) + [
-            pltpu.VMEM((n, 8, 128), jnp.int32),
-            pltpu.SMEM((n, 8, 128), jnp.int32),
-            pltpu.VMEM((n, half_rows, E), bf16),
-            pltpu.VMEM((n, half_rows, E), bf16),
-            pltpu.VMEM((span_count, half_rows, E), bf16),
-            pltpu.VMEM((rows, E), bf16),
-            pltpu.VMEM((2, E, tokens), bf16),
-            pltpu.VMEM((E, E), bf16),
-            pltpu.VMEM((E, E), bf16),
-            pltpu.VMEM((rows, E), bf16),
-            pltpu.VMEM((rows, E), bf16),
-            dma((7,)),
-            dma((2, n)),
-            dma((2, n)),
-            dma((2, span_count)),
-            dma((2, 4)),
-            dma((2,)),
-            dma((2, 2, n // 2)),
-            dma((2, 2, n // 2)),
-        ],
-        nb, passages.reshape(-1, 2, half_rows, E), memory, enc_query_w.T, enc_out_w.T, kv, span_queries,
+        [states] if fused else [sds(enc_shape, bf16), sds(kv_shape, bf16)],
+        scratch, [pltpu.VMEM] + [pl.ANY] * 8,
+        neighbours, passages.reshape(-1, 2, half_rows, E), memory, enc_query_w.T, enc_out_w.T, kv,
+        span_queries, out_weight, span_states,
     )
-    attended = found[0] if fused else decode(found[0], found[1], span_queries, span_count)
-    rows, width = tokens, out_weight.shape[1]
-    return vmem_call(
-        functools.partial(out_kernel, n), 1,
-        sds(span_states.shape, bf16),
-        [
-            pltpu.VMEM((n,) + attended.shape, bf16),
-            pltpu.VMEM((n, 2, rows // 2, width), bf16),
-            pltpu.VMEM((n, rows // 2, width), bf16),
-            pltpu.VMEM((n, rows // 2, width), bf16),
-            pltpu.VMEM((n // 2, 2, rows // 2, width), bf16),
-            dma((2, 2, n // 2)),
-            dma((2, n)),
-            dma((n,)),
-            dma((n // 2, 2)),
-            dma((1,)),
-        ],
+    if fused:
+        return found[0]
+    attended = decode(found[0], found[1], span_queries, span_count)
+    return call(
+        functools.partial(out_kernel, n), 1, [states], out_scratch, [pltpu.VMEM] * 3,
         attended, out_weight, span_states,
-    )
+    )[0]
 
 
 def solution(mesh):

time: 126 us -> 105 us (0.83)
  Pallas kernels: 121 us -> 101 us
  local copies, waits for them, and re-layouts: 5.08 us -> 3.73 us
    pallas_call x2 -> x1, Pallas kernels: 121 us -> 101 us  [call(): pl.pallas_call(kernel, out_shape=out_shape, in_specs=[pl.BlockSpec(memory...]
where the time goes in v3:
time: 105 us
  Pallas kernels  101 us (96%)
  local copies, waits for them, and re-layouts  3.73 us (4%)
    pallas_call x1, Pallas kernels, call(): pl.pallas_call(kernel, out_shape=out_shape, in_specs=[pl.BlockSpec(memory...  101 us
    unnamed x2, local copies, waits for them, and re-layouts  3.73 us

profile of v3, /device:TPU:1, one launch (start us, length us, event | category | flops | bytes accessed | tf_op | source)
XLA Modules:
  0.0 105.0 jit_solution(2350293984804106252)
XLA Ops:
  0.0 1.8 %copy.12 = bf16[896,2,128]{2,0,1:T(8,128)(2,1)} copy(bf16[896,2,128]{2,1,0:T(2,128)(2,1)} %param.16) | data formatting | bytes 917504 | tf_op args[7]
  1.8 101.2 %shard_map.91 = bf16[128,2048]{1,0:T(8,128)(2,1)} custom-call(s32[2,2]{1,0:T(2,128)} %nb_ref.1, bf16[8,2,64,896]{3,2,1,0:T(8,128)(2,1)} %bitcast.8, bf16[2,448,128]{2,1,0:T(8,128)(2,1)} %bitcast.11, bf16[448,896]{1,0:T(8,128)(2,1)} %bitcast.9, bf16[448,896]{1,0:T(8,128)(2,1)} %bitcast.10, bf16[2,896,128]{2,1,0:T(8,128)(2,1)} %bitcast.7, ...), custom_call_target="tpu_custom_call" | custom-call | tf_op jit(solution)/shard_map/pallas_call | solution.py:409
  103.1 1.9 %copy.14 = bf16[128,2048]{1,0:T(8,128)(2,1)} copy(bf16[128,2048]{1,0:T(8,128)(2,1)} %shard_map.91) | data formatting | bytes 1048576

commit v4 on v3

--- a/solution.py
+++ b/solution.py
@@ -170,7 +170,7 @@
     own_nb.start()
 
     depth = kv_ref.shape[1]
-    half, extra = depth // 2, depth // 4
+    half, extra = depth // 2, depth // 28 * 3
     near, far = part, 1 - part
 
     def pieces(ref):
@@ -247,6 +247,7 @@
     for copy in swaps:
         copy.wait()
 
+    arrivals.append(ring.advance(1, to_twin))
     rows = cop.shape[0]
     tokens = mem.shape[2]
     width = cop.shape[1]
@@ -264,7 +265,6 @@
             term = dot(weigh(scores, mask), vals, ((1,), (1,)))
             total = term if e == 0 else total + term
         mixed[:, lines] = total.astype(jnp.bfloat16)
-    arrivals.append(ring.advance(1, to_twin))
     branch = dot(mixed[...], wo[...])
     enc[head] = rms_rows(cop[...].astype(jnp.float32) + branch).astype(jnp.bfloat16)
     enc_copy = remote(enc.at[head], enc.at[head], enc_sem.at[0], enc_sem.at[1], head=other)

time: 105 us -> 105 us (level)
  no operation moved by 1% of the time
where the time goes in v4:
time: 105 us
  Pallas kernels  101 us (96%)
  local copies, waits for them, and re-layouts  3.73 us (4%)
    pallas_call x1, Pallas kernels, call(): pl.pallas_call(kernel, out_shape=out_shape, in_specs=[pl.BlockSpec(memory...  101 us
    unnamed x2, local copies, waits for them, and re-layouts  3.73 us

profile of v4, /device:TPU:1, one launch (start us, length us, event | category | flops | bytes accessed | tf_op | source)
XLA Modules:
  0.0 104.5 jit_solution(6768648055684066361)
XLA Ops:
  0.0 1.8 %copy.12 = bf16[896,2,128]{2,0,1:T(8,128)(2,1)} copy(bf16[896,2,128]{2,1,0:T(2,128)(2,1)} %param.16) | data formatting | bytes 917504 | tf_op args[7]
  1.8 100.8 %shard_map.91 = bf16[128,2048]{1,0:T(8,128)(2,1)} custom-call(s32[2,2]{1,0:T(2,128)} %nb_ref.1, bf16[8,2,64,896]{3,2,1,0:T(8,128)(2,1)} %bitcast.8, bf16[2,448,128]{2,1,0:T(8,128)(2,1)} %bitcast.11, bf16[448,896]{1,0:T(8,128)(2,1)} %bitcast.9, bf16[448,896]{1,0:T(8,128)(2,1)} %bitcast.10, bf16[2,896,128]{2,1,0:T(8,128)(2,1)} %bitcast.7, ...), custom_call_target="tpu_custom_call" | custom-call | tf_op jit(solution)/shard_map/pallas_call | solution.py:409
  102.7 1.9 %copy.14 = bf16[128,2048]{1,0:T(8,128)(2,1)} copy(bf16[128,2048]{1,0:T(8,128)(2,1)} %shard_map.91) | data formatting | bytes 1048576

commit v5 on v4

--- a/solution.py
+++ b/solution.py
@@ -291,8 +291,8 @@
         attend(me)
 
     for t in range(ring.steps):
-        if t >= len(arrivals):
-            arrivals.append(ring.advance(t, to_twin))
+        while len(arrivals) < min(t + 3, ring.steps):
+            arrivals.append(ring.advance(len(arrivals), to_twin))
         for copy in twins[t]:
             copy.wait_recv()
         if fused:

time: 105 us -> 102 us (0.971)
  Pallas kernels: 101 us -> 98.1 us
    pallas_call x1, Pallas kernels: 101 us -> 98.1 us  [call(): pl.pallas_call(kernel, out_shape=out_shape, in_specs=[pl.BlockSpec(memory...]
where the time goes in v5:
time: 102 us
  Pallas kernels  98.1 us (96%)
  local copies, waits for them, and re-layouts  3.73 us (4%)
    pallas_call x1, Pallas kernels, call(): pl.pallas_call(kernel, out_shape=out_shape, in_specs=[pl.BlockSpec(memory...  98.1 us
    unnamed x2, local copies, waits for them, and re-layouts  3.73 us

profile of v5, /device:TPU:1, one launch (start us, length us, event | category | flops | bytes accessed | tf_op | source)
XLA Modules:
  0.0 101.9 jit_solution(8257248579025533779)
XLA Ops:
  0.0 1.8 %copy.12 = bf16[896,2,128]{2,0,1:T(8,128)(2,1)} copy(bf16[896,2,128]{2,1,0:T(2,128)(2,1)} %param.16) | data formatting | bytes 917504 | tf_op args[7]
  1.8 98.1 %shard_map.91 = bf16[128,2048]{1,0:T(8,128)(2,1)} custom-call(s32[2,2]{1,0:T(2,128)} %nb_ref.1, bf16[8,2,64,896]{3,2,1,0:T(8,128)(2,1)} %bitcast.8, bf16[2,448,128]{2,1,0:T(8,128)(2,1)} %bitcast.11, bf16[448,896]{1,0:T(8,128)(2,1)} %bitcast.9, bf16[448,896]{1,0:T(8,128)(2,1)} %bitcast.10, bf16[2,896,128]{2,1,0:T(8,128)(2,1)} %bitcast.7, ...), custom_call_target="tpu_custom_call" | custom-call | tf_op jit(solution)/shard_map/pallas_call | solution.py:409
  100.0 1.9 %copy.14 = bf16[128,2048]{1,0:T(8,128)(2,1)} copy(bf16[128,2048]{1,0:T(8,128)(2,1)} %shard_map.91) | data formatting | bytes 1048576
